TPU v7x, 32 devices: a whole 2x2x4 slice. The times are simulated.
32 devices in a mesh: fsdp: 4 (over z), ctx: 8 (over y, x, core).
Axes of the slice: x: 2, y: 2, z: 4, core: 2. Of those that a mesh axis runs over, the one named last changes fastest.
Arguments:
- hidden_in: bfloat16 [4, 1024, 1024], P('fsdp', 'ctx'), may hold values from -6 to 6
- pair_table: int32 [8, 2], replicated, may hold values from 0 to 15, as said below
- attn_gain: float32 [1024], replicated, may hold values from 0.5 to 1.5
- query_proj: bfloat16 [1024, 2048], P('fsdp'), may hold values from -0.1875 to 0.1875
- key_proj: bfloat16 [1024, 1024], P('fsdp'), may hold values from -0.1875 to 0.1875
- value_proj: bfloat16 [1024, 1024], P('fsdp'), may hold values from -0.1875 to 0.1875
- query_gain: float32 [128], replicated, may hold values from 0.6 to 5
- key_gain: float32 [128], replicated, may hold values from 0.6 to 5
- output_proj: bfloat16 [1024, 2048], P('fsdp'), may hold values from -2 to 2
- mlp_gain: float32 [1024], replicated, may hold values from 0.5 to 1.5
- gate_proj: bfloat16 [1024, 3072], P('fsdp'), may hold values from -0.1875 to 0.1875
- up_proj: bfloat16 [1024, 3072], P('fsdp'), may hold values from -0.1875 to 0.1875
- down_proj: bfloat16 [1024, 3072], P('fsdp'), may hold values from -0.109375 to 0.109375
- cotangent: bfloat16 [4, 1024, 1024], P('fsdp', 'ctx'), may hold values from -6 to 6
Outputs:
- block_out: bfloat16 [4, 1024, 1024], P('fsdp', 'ctx')
- input_grad: float32 [4, 1024, 1024], P('fsdp', 'ctx')
- attn_gain_grad: float32 [1024], replicated
- query_proj_grad: float32 [1024, 2048], P('fsdp')
- key_proj_grad: float32 [1024, 1024], P('fsdp')
- value_proj_grad: float32 [1024, 1024], P('fsdp')
- query_gain_grad: float32 [128], replicated
- key_gain_grad: float32 [128], replicated
- output_proj_grad: float32 [1024, 2048], P('fsdp')
- mlp_gain_grad: float32 [1024], replicated
- gate_proj_grad: float32 [1024, 3072], P('fsdp')
- up_proj_grad: float32 [1024, 3072], P('fsdp')
- down_proj_grad: float32 [1024, 3072], P('fsdp')
Inputs may be any that keep to these rules, and one draw needn't show every extreme that they name: `pair_table`: row c is (p, 15 - p); the p of the rows are 0 to 7, each once.
All inputs are finite; a program needn't handle non-finite values.
Results may differ from a plain program's by a relative error of at most 0.028.
The roundings to bfloat16 on the way count: a program that leaves them out, or rounds other values in their place, can miss the bound.
Values may be sent and summed in bfloat16 or wider, within the bound.
No kernel may reach another device: no remote copies, remote signals or barrier semaphores. Data moves between devices by JAX's collectives and lax.ppermute only.
A program may use at most 320 MiB of HBM per device.

v0:
```python
import math
import jax
import jax.numpy as jnp
from jax import lax
from jax.sharding import PartitionSpec as P

NORM_EPS = 1e-06
ROPE_BASE = 1000000.0
MASKED = -1e30


def rms_norm(values, gain_vec):
    return (
        values * lax.rsqrt(jnp.mean(values * values, axis=-1, keepdims=True) + NORM_EPS) * gain_vec
    )


def rotate(values, angles):
    half_width = values.shape[-1] // 2
    cosine = jnp.cos(angles)[:, None, :]
    sine_part = jnp.sin(angles)[:, None, :]
    first_half = values[..., :half_width]
    second_half = values[..., half_width:]
    return jnp.concatenate(
        [
            first_half * cosine - second_half * sine_part,
            second_half * cosine + first_half * sine_part,
        ],
        axis=-1,
    )


def head_prep(raw_heads, gain_vec, angles):
    return rotate(rms_norm(raw_heads, gain_vec), angles)


def angle_table(positions, head_width):
    half_width = head_width // 2
    frequency = ROPE_BASE ** (-(jnp.arange(half_width, dtype=jnp.float32) * 2.0 / head_width))
    return positions.astype(jnp.float32)[:, None] * frequency[None, :]


def token_positions(pair_table, row_count, block_len):
    index_rows = jnp.arange(row_count, dtype=jnp.int32)
    owners = index_rows // (2 * block_len)
    halves = index_rows // block_len % 2
    return pair_table[owners, halves] * block_len + index_rows % block_len


def times_transposed(lhs_mat, rhs_mat):
    return lax.dot_general(
        lhs_mat, rhs_mat, (((1,), (1,)), ((), ())), preferred_element_type=jnp.float32
    )


def transposed_times(lhs_mat, rhs_mat):
    return lax.dot_general(
        lhs_mat, rhs_mat, (((0,), (0,)), ((), ())), preferred_element_type=jnp.float32
    )


def block_scores(grouped_query, key_blk, query_pos, key_pos_blk, score_scale):
    raw_scores = (
        jnp.einsum("qhgd,khd->hgqk", grouped_query, key_blk, preferred_element_type=jnp.float32)
        * score_scale
    )
    allowed = key_pos_blk[None, :] <= query_pos[:, None]
    return (jnp.where(allowed[None, None], raw_scores, MASKED), allowed)


def on_device(
    hidden_in,
    pair_table,
    attn_gain,
    query_proj,
    key_proj,
    value_proj,
    query_gain,
    key_gain,
    output_proj,
    mlp_gain,
    gate_proj,
    up_proj,
    down_proj,
    cotangent,
):
    query_w, key_w, value_w, output_w = (
        lax.all_gather(query_proj, "fsdp", axis=0, tiled=True),
        lax.all_gather(key_proj, "fsdp", axis=0, tiled=True),
        lax.all_gather(value_proj, "fsdp", axis=0, tiled=True),
        lax.all_gather(output_proj, "fsdp", axis=0, tiled=True),
    )
    gate_w, upper_w, down_w = (
        lax.all_gather(gate_proj, "fsdp", axis=0, tiled=True),
        lax.all_gather(up_proj, "fsdp", axis=0, tiled=True),
        lax.all_gather(down_proj, "fsdp", axis=0, tiled=True),
    )
    inputs = hidden_in[0]
    cot_low = cotangent[0]
    row_count = inputs.shape[0]
    block_len = row_count // 2
    ctx_count = lax.axis_size("ctx")
    ctx_index = lax.axis_index("ctx")
    head_width = query_gain.shape[0]
    query_count = query_w.shape[1] // head_width
    kvhead_count = key_w.shape[1] // head_width
    group_size = query_count // kvhead_count
    score_scale = 1.0 / math.sqrt(head_width)
    local_rows = jnp.arange(block_len, dtype=jnp.int32)
    own_pos = jnp.concatenate(
        [
            pair_table[ctx_index, 0] * block_len + local_rows,
            pair_table[ctx_index, 1] * block_len + local_rows,
        ]
    )
    total_keys = ctx_count * row_count
    key_pos = token_positions(pair_table, total_keys, block_len)
    key_block = math.gcd(total_keys, 512)
    block_count = total_keys // key_block
    angles = angle_table(own_pos, head_width)

    def head_query(raw_heads, gain_vec):
        return head_prep(raw_heads, gain_vec, angles)

    input_wide = inputs.astype(jnp.float32)
    attn_in = rms_norm(input_wide, attn_gain).astype(jnp.bfloat16)
    query_raw = jnp.dot(attn_in, query_w, preferred_element_type=jnp.float32).reshape(
        row_count, query_count, head_width
    )
    key_raw = jnp.dot(attn_in, key_w, preferred_element_type=jnp.float32).reshape(
        row_count, kvhead_count, head_width
    )
    value_raw = jnp.dot(attn_in, value_w, preferred_element_type=jnp.float32)
    query_heads = head_query(query_raw, query_gain).astype(jnp.bfloat16)
    key_heads = head_query(key_raw, key_gain).astype(jnp.bfloat16)
    value_heads = value_raw.astype(jnp.bfloat16)
    key_all, value_all = (
        lax.all_gather(key_heads.reshape(row_count, -1), "ctx", axis=0, tiled=True),
        lax.all_gather(value_heads, "ctx", axis=0, tiled=True),
    )
    key_blocks = key_all.reshape(block_count, key_block, kvhead_count, head_width)
    value_blocks = value_all.reshape(block_count, key_block, kvhead_count, head_width)
    pos_blocks = key_pos.reshape(block_count, key_block)
    grouped_query = query_heads.reshape(row_count, kvhead_count, group_size, head_width)

    def stats_step(state_pair, block_data):
        running_max, running_sum = state_pair
        key_blk, pos_blk = block_data
        scores, allowed = block_scores(grouped_query, key_blk, own_pos, pos_blk, score_scale)
        new_max = jnp.maximum(running_max, jnp.max(scores, axis=-1))
        weights_now = jnp.where(allowed[None, None], jnp.exp(scores - new_max[..., None]), 0.0)
        running_sum = running_sum * jnp.exp(running_max - new_max) + jnp.sum(weights_now, axis=-1)
        return ((new_max, running_sum), None)

    stat_shape = (kvhead_count, group_size, row_count)
    (row_max, row_sum), unused = lax.scan(
        stats_step,
        (jnp.full(stat_shape, MASKED, jnp.float32), jnp.zeros(stat_shape, jnp.float32)),
        (key_blocks, pos_blocks),
    )
    log_total = row_max + jnp.log(row_sum)

    def mix_step(accum, block_data):
        key_blk, value_blk, pos_blk = block_data
        scores, allowed = block_scores(grouped_query, key_blk, own_pos, pos_blk, score_scale)
        probs = jnp.exp(scores - log_total[..., None]).astype(jnp.bfloat16)
        return (
            accum
            + jnp.einsum("hgqk,khd->qhgd", probs, value_blk, preferred_element_type=jnp.float32),
            None,
        )

    mixed, unused = lax.scan(
        mix_step,
        jnp.zeros((row_count, kvhead_count, group_size, head_width), jnp.float32),
        (key_blocks, value_blocks, pos_blocks),
    )
    attn_mix = mixed.reshape(row_count, -1).astype(jnp.bfloat16)
    resid = input_wide + times_transposed(attn_mix, output_w)
    mlp_in = rms_norm(resid, mlp_gain).astype(jnp.bfloat16)
    gate = jnp.dot(mlp_in, gate_w, preferred_element_type=jnp.float32)
    upper = jnp.dot(mlp_in, upper_w, preferred_element_type=jnp.float32)
    sigma = jax.nn.sigmoid(gate)
    hidden_act = (gate * sigma * upper).astype(jnp.bfloat16)
    block_out = (resid + times_transposed(hidden_act, down_w)).astype(jnp.bfloat16)
    hidden_grad = jnp.dot(cot_low, down_w, preferred_element_type=jnp.float32)
    gate_low = (hidden_grad * upper * sigma * (1.0 + gate * (1.0 - sigma))).astype(jnp.bfloat16)
    upper_low = (hidden_grad * gate * sigma).astype(jnp.bfloat16)
    mlp_in_grad = times_transposed(gate_low, gate_w) + times_transposed(upper_low, upper_w)
    resid_part, mlp_gain_grad = jax.vjp(rms_norm, resid, mlp_gain)[1](mlp_in_grad)
    resid_grad = cot_low.astype(jnp.float32) + resid_part
    resid_low = resid_grad.astype(jnp.bfloat16)
    mix_grad = jnp.dot(resid_low, output_w, preferred_element_type=jnp.float32).astype(jnp.bfloat16)
    dmix_heads = mix_grad.reshape(row_count, kvhead_count, group_size, head_width)
    delta = jnp.einsum(
        "qhgd,qhgd->hgq",
        dmix_heads,
        attn_mix.reshape(row_count, kvhead_count, group_size, head_width),
        preferred_element_type=jnp.float32,
    )

    def grad_step(query_accum, block_data):
        key_blk, value_blk, pos_blk = block_data
        scores, allowed = block_scores(grouped_query, key_blk, own_pos, pos_blk, score_scale)
        probs = jnp.exp(scores - log_total[..., None])
        value_part = jnp.einsum(
            "hgqk,qhgd->khd",
            probs.astype(jnp.bfloat16),
            dmix_heads,
            preferred_element_type=jnp.float32,
        )
        prob_grad = jnp.einsum(
            "qhgd,khd->hgqk", dmix_heads, value_blk, preferred_element_type=jnp.float32
        )
        score_grad = (probs * (prob_grad - delta[..., None]) * score_scale).astype(jnp.bfloat16)
        query_accum = query_accum + jnp.einsum(
            "hgqk,khd->qhgd", score_grad, key_blk, preferred_element_type=jnp.float32
        )
        key_part = jnp.einsum(
            "hgqk,qhgd->khd", score_grad, grouped_query, preferred_element_type=jnp.float32
        )
        return (query_accum, (key_part, value_part))

    query_grad, (key_parts, value_parts) = lax.scan(
        grad_step,
        jnp.zeros((row_count, kvhead_count, group_size, head_width), jnp.float32),
        (key_blocks, value_blocks, pos_blocks),
    )
    key_grad, value_grad = (
        lax.psum_scatter(
            key_parts.reshape(total_keys, -1).astype(jnp.bfloat16),
            "ctx",
            scatter_dimension=0,
            tiled=True,
        ).astype(jnp.float32),
        lax.psum_scatter(
            value_parts.reshape(total_keys, -1).astype(jnp.bfloat16),
            "ctx",
            scatter_dimension=0,
            tiled=True,
        ).astype(jnp.float32),
    )
    query_raw_grad, query_gain_grad = jax.vjp(head_query, query_raw, query_gain)[1](
        query_grad.reshape(row_count, query_count, head_width)
    )
    key_raw_grad, key_gain_grad = jax.vjp(head_query, key_raw, key_gain)[1](
        key_grad.reshape(row_count, kvhead_count, head_width)
    )
    query_low = query_raw_grad.reshape(row_count, -1).astype(jnp.bfloat16)
    key_low = key_raw_grad.reshape(row_count, -1).astype(jnp.bfloat16)
    value_low = value_grad.astype(jnp.bfloat16)
    attn_in_grad = (
        times_transposed(query_low, query_w)
        + times_transposed(key_low, key_w)
        + times_transposed(value_low, value_w)
    )
    input_part, attn_gain_grad = jax.vjp(rms_norm, input_wide, attn_gain)[1](attn_in_grad)
    input_grad = resid_grad + input_part
    attn_right = jnp.concatenate([query_low, key_low, value_low], axis=1)
    mlp_right = jnp.concatenate([gate_low, upper_low], axis=1)
    pairings = (
        (attn_in, attn_right),
        (resid_low, attn_mix),
        (mlp_in, mlp_right),
        (cot_low, hidden_act),
    )
    pieces = [transposed_times(operand, partner) for operand, partner in pairings]
    owned_term = lax.psum_scatter(
        jnp.concatenate(pieces, axis=1).astype(jnp.bfloat16),
        "fsdp",
        scatter_dimension=0,
        tiled=True,
    )
    owned = lax.psum(owned_term, "ctx").astype(jnp.float32)
    attn_gain_grad, query_gain_grad, key_gain_grad, mlp_gain_grad = lax.psum(
        (attn_gain_grad, query_gain_grad, key_gain_grad, mlp_gain_grad), ("fsdp", "ctx")
    )
    widths = (
        query_w.shape[1],
        key_w.shape[1],
        value_w.shape[1],
        output_w.shape[1],
        gate_w.shape[1],
        upper_w.shape[1],
        down_w.shape[1],
    )
    offsets = [0]
    for column_count in widths:
        offsets.append(offsets[-1] + column_count)
    grads = [owned[:, offsets[number] : offsets[number + 1]] for number in range(len(widths))]
    return (
        block_out[None],
        input_grad[None],
        attn_gain_grad,
        grads[0],
        grads[1],
        grads[2],
        query_gain_grad,
        key_gain_grad,
        grads[3],
        mlp_gain_grad,
        grads[4],
        grads[5],
        grads[6],
    )


def solution(mesh):
    in_specs = (
        P("fsdp", "ctx", None),
        P(),
        P(),
        P("fsdp", None),
        P("fsdp", None),
        P("fsdp", None),
        P(),
        P(),
        P("fsdp", None),
        P(),
        P("fsdp", None),
        P("fsdp", None),
        P("fsdp", None),
        P("fsdp", "ctx", None),
    )
    out_specs = (
        P("fsdp", "ctx", None),
        P("fsdp", "ctx", None),
        P(),
        P("fsdp", None),
        P("fsdp", None),
        P("fsdp", None),
        P(),
        P(),
        P("fsdp", None),
        P(),
        P("fsdp", None),
        P("fsdp", None),
        P("fsdp", None),
    )
    return jax.shard_map(
        on_device, mesh=mesh, in_specs=in_specs, out_specs=out_specs, check_vma=False
    )
```

profile of v0, /device:TPU:0, one launch (start us, length us, event | category | flops | bytes accessed | tf_op | source)
XLA Modules:
  0.0 1498.1 jit_solution(4632809275431126359)
XLA Ops:
  10.6 47.4 %all-gather.10.cloned.1.call-done = bf16[1024,1024]{1,0:T(8,128)(2,1)} async-done(((bf16[256,1024]{1,0:T(8,128)(2,1)}), bf16[1024,1024]{1,0:T(8,128)(2,1)}) %all-gather.10.cloned.1.call-update) | async-done | bytes 2097168 | tf_op jit(solution)/shard_map/all_gather | solution.py:90
  63.2 40.9 %all-gather.14.cloned.1.call-done = bf16[1024,1024]{1,0:T(8,128)(2,1)} async-done(((bf16[256,1024]{1,0:T(8,128)(2,1)}), bf16[1024,1024]{1,0:T(8,128)(2,1)}) %all-gather.14.cloned.1.call-update) | async-done | bytes 2097168 | tf_op jit(solution)/shard_map/all_gather | solution.py:89
  104.0 3.9 copy.60
  114.5 8.8 gather_fusion
  123.4 61.8 %all-gather.18.cloned.1.call-done = bf16[1024,2048]{1,0:T(8,128)(2,1)} async-done(((bf16[256,2048]{1,0:T(8,128)(2,1)}), bf16[1024,2048]{1,0:T(8,128)(2,1)}) %all-gather.18.cloned.1.call-update) | async-done | bytes 4194320 | tf_op jit(solution)/shard_map/all_gather | solution.py:88
  185.2 6.4 copy.62
  197.6 16.2 %all-gather.12.cloned.1.call-done = bf16[1024,1024]{1,0:T(8,128)(2,1)} async-done(((bf16[128,1024]{1,0:T(8,128)(2,1)}), bf16[1024,1024]{1,0:T(8,128)(2,1)}) %all-gather.12.cloned.1.call-update) | async-done | bytes 2097168 | tf_op jit(solution)/shard_map/all_gather | solution.py:139
  217.4 26.6 %all-gather.16.cloned.1.call-done = bf16[1024,1024]{1,0:T(8,128)(2,1)} async-done(((bf16[128,1024]{1,0:T(8,128)(2,1)}), bf16[1024,1024]{1,0:T(8,128)(2,1)}) %all-gather.16.cloned.1.call-update) | async-done | bytes 2097168 | tf_op jit(solution)/shard_map/all_gather | solution.py:138
  246.5 4.0 while.39
  250.6 17.8 %while.40 = (s32[]{:T(128)}, f32[128,8,2,128]{0,3,2,1:T(8,128)}, bf16[2,512,8,128]{3,2,1,0:T(8,128)(2,1)}, s32[2,512]{1,0:T(2,128)S(1)}, s32[128]{0:T(128)S(1)},...) while((s32[]{:T(128)}, f32[128,8,2,128]{0,3,2,1:T(8,128)}, ...), condition=%wide.region_8.9_spmd.clone, body=%wide.region_7.8_spmd.clone.sunk | while | flops 541655040 | bytes 9058947 | solution.py:173
  270.5 55.6 %all-gather.20.cloned.1.call-done = bf16[1024,2048]{1,0:T(8,128)(2,1)} async-done(((bf16[256,2048]{1,0:T(8,128)(2,1)}), bf16[1024,2048]{1,0:T(8,128)(2,1)}) %all-gather.20.cloned.1.call-update) | async-done | bytes 4194320 | tf_op jit(solution)/shard_map/all_gather | solution.py:91
  326.1 3.9 multiply_reduce_fusion.8
  330.9 110.6 %all-gather.24.cloned.1.call-done = bf16[1024,3072]{1,0:T(8,128)(2,1)} async-done(((bf16[256,3072]{1,0:T(8,128)(2,1)}), bf16[1024,3072]{1,0:T(8,128)(2,1)}) %all-gather.24.cloned.1.call-update) | async-done | bytes 6291472 | tf_op jit(solution)/shard_map/all_gather | solution.py:95
  441.5 5.0 fusion.105
  446.6 110.1 %all-gather.22.cloned.1.call-done = bf16[1024,3072]{1,0:T(8,128)(2,1)} async-done(((bf16[256,3072]{1,0:T(8,128)(2,1)}), bf16[1024,3072]{1,0:T(8,128)(2,1)}) %all-gather.22.cloned.1.call-update) | async-done | bytes 6291472 | tf_op jit(solution)/shard_map/all_gather | solution.py:94
  556.7 5.0 fusion.104
  561.7 110.1 %all-gather.26.cloned.1.call-done = bf16[1024,3072]{1,0:T(8,128)(2,1)} async-done(((bf16[256,3072]{1,0:T(8,128)(2,1)}), bf16[1024,3072]{1,0:T(8,128)(2,1)}) %all-gather.26.cloned.1.call-update) | async-done | bytes 6291472 | tf_op jit(solution)/shard_map/all_gather | solution.py:96
  671.8 6.5 multiply_convert_fusion
  680.6 5.3 multiply_reduce_fusion.4
  698.9 19.8 %while.41 = (s32[]{:T(128)}, f32[128,8,2,128]{0,3,2,1:T(8,128)}, bf16[2,512,8,128]{3,1,2,0:T(8,128)(2,1)}, bf16[2,512,8,128]{3,1,2,0:T(8,128)(2,1)}, bf16[2,512,...) while((s32[]{:T(128)}, f32[128,8,2,128]{0,3,2,1:T(8,128)}, ...), condition=%wide.region_12.13_spmd.clone, body=%wide.region_11.12_spmd.clone.sunk | while | flops 1354301440 | bytes 76774256 | solution.py:224
  735.7 4.5 convert_bitcast_fusion
  740.2 6.6 convolution_convert_fusion
  746.8 16.2 %reduce-scatter.6.cloned.1.call-done = bf16[128,1024]{1,0:T(8,128)(2,1)} async-done(((bf16[1024,1024]{1,0:T(8,128)(2,1)}), bf16[128,1024]{1,0:T(8,128)(2,1)}) %reduce-scatter.6.cloned.1.call-update) | async-done | bytes 262160 | tf_op jit(solution)/shard_map/reduce_scatter | solution.py:230
  765.3 42.7 %reduce-scatter.8.cloned.1.call-done = bf16[128,1024]{1,0:T(8,128)(2,1)} async-done(((bf16[1024,1024]{1,0:T(8,128)(2,1)}), bf16[128,1024]{1,0:T(8,128)(2,1)}) %reduce-scatter.8.cloned.1.call-update) | async-done | bytes 262160 | tf_op jit(solution)/shard_map/reduce_scatter | solution.py:236
  809.2 7.1 convolution_convert_fusion.1
  816.3 19.7 %pad_maximum_fusion = bf16[1024,15360]{1,0:T(8,128)(2,1)} fusion(bf16[1024,3072]{1,0:T(8,128)(2,1)S(1)} %bitcast.290, bf16[1024,6144]{1,0:T(8,128)(2,1)} %convolution_convert_fusion, bf16[1024,2048]{1,0:T(8,128)(2,1)} %convolution_convert_fusion.2, bf16[1024,4096]{1,0:T(8,128)(2,1)} %convolution_convert_fusion.1), kind=kLoop, calls=%fused_computation.60 | loop fusion | flops 125829120 | bytes 62914560 | tf_op jit(solution)/shard_map/concatenate | solution.py:269
  836.3 515.3 %reduce-scatter.10.cloned.1.call-done = bf16[256,15360]{1,0:T(8,128)(2,1)} async-done(((bf16[1024,15360]{1,0:T(8,128)(2,1)}), bf16[256,15360]{1,0:T(8,128)(2,1)}) %reduce-scatter.10.cloned.1.call-update) | async-done | bytes 7864336
  1351.7 5.8 fusion.51
  1361.5 43.2 %all-reduce.5 = (f32[1024]{0:T(1024)}, f32[128]{0:T(128)}, f32[128]{0:T(128)}, f32[1024]{0:T(1024)}) all-reduce(f32[1024]{0:T(1024)S(1)} %get-tuple-element.333, f32[128]{0:T(128)S(1)} %get-tuple-element.327, f32[128]{0:T(128)S(1)} %get-tuple-element.331, ...), channel_id=1, replica_groups=mesh['fsdp'=4,'ctx'=8] {'fsdp','ctx'}, use_global_device_ids=true, to_apply=%region_19.20 | all-reduce | flops 2304 | bytes 18432 | tf_op jit(solution)/shard_map/psum | solution.py:275
  1405.7 73.3 %all-reduce.8.cloned.1.call-done = bf16[256,15360]{1,0:T(8,128)(2,1)} async-done(((bf16[256,15360]{1,0:T(8,128)(2,1)}), bf16[256,15360]{1,0:T(8,128)(2,1)}) %all-reduce.8.cloned.1.call-update) | async-done | bytes 7864336 | tf_op jit(solution)/shard_map/psum | solution.py:274
  1481.8 4.4 fusion.102
  1487.2 4.1 fusion.101
  (237 shorter events, 113.6 us)
Async XLA Ops:
  7.2 53.8 %copy-start = (s32[8,2]{0,1:T(2,128)S(1)}, s32[8,2]{0,1:T(2,128)}, u32[]{:S(2)}) copy-start(s32[8,2]{0,1:T(2,128)} %param.21) | copy-start | bytes 196
  7.2 50.8 %all-gather.10.cloned.1.call-start = ((), (), s32[]{:S(2)}) async-start(), calls=%async_computation.3 | async-start | bytes 2621440 | tf_op jit(solution)/shard_map/all_gather | solution.py:90
  7.9 96.1 %all-gather.14.cloned.1.call-start = ((), (), s32[]{:S(2)}) async-start(), calls=%async_computation.5 | async-start | bytes 2621440 | tf_op jit(solution)/shard_map/all_gather | solution.py:89
  8.7 99.3 %copy-start.6 = (bf16[1,128,1024]{2,1,0:T(8,128)(2,1)S(1)}, bf16[1,128,1024]{2,1,0:T(8,128)(2,1)}, u32[]{:S(2)}) copy-start(bf16[1,128,1024]{2,1,0:T(8,128)(2,1)} %param.20) | copy-start | bytes 786436
  8.7 99.3 %copy-start.36 = (f32[1024]{0:T(1024)S(1)}, f32[1024]{0:T(1024)}, u32[]{:S(2)}) copy-start(f32[1024]{0:T(1024)} %param.22) | copy-start | bytes 12292
  8.7 176.5 %all-gather.18.cloned.1.call-start = ((), (), s32[]{:S(2)}) async-start(), calls=%async_computation.7 | async-start | bytes 5242880 | tf_op jit(solution)/shard_map/all_gather | solution.py:88
  9.4 204.4 %all-gather.12.cloned.1.call-start = ((), (), s32[]{:S(2)}) async-start(), calls=%async_computation.4 | async-start | bytes 2359296 | tf_op jit(solution)/shard_map/all_gather | solution.py:139
  10.6 52.3 %copy-start.40 = (f32[128]{0:T(128)}, f32[128]{0:T(128)S(1)}, u32[]{:S(2)}) copy-start(f32[128]{0:T(128)S(1)} %fusion.66) | copy-start | bytes 1540
  60.9 49.5 %copy-start.38 = (f32[128]{0:T(128)S(1)}, f32[128]{0:T(128)}, u32[]{:S(2)}) copy-start(f32[128]{0:T(128)} %param.27) | copy-start | bytes 1540
  60.9 183.0 %all-gather.16.cloned.1.call-start = ((), (), s32[]{:S(2)}) async-start(), calls=%async_computation.6 | async-start | bytes 2359296 | tf_op jit(solution)/shard_map/all_gather | solution.py:138
  111.5 214.6 %all-gather.20.cloned.1.call-start = ((), (), s32[]{:S(2)}) async-start(), calls=%async_computation.8 | async-start | bytes 5242880 | tf_op jit(solution)/shard_map/all_gather | solution.py:91
  112.1 329.5 %all-gather.24.cloned.1.call-start = ((), (), s32[]{:S(2)}) async-start(), calls=%async_computation.10 | async-start | bytes 7864320 | tf_op jit(solution)/shard_map/all_gather | solution.py:95
  112.8 443.8 %all-gather.22.cloned.1.call-start = ((), (), s32[]{:S(2)}) async-start(), calls=%async_computation.9 | async-start | bytes 7864320 | tf_op jit(solution)/shard_map/all_gather | solution.py:94
  113.6 558.2 %all-gather.26.cloned.1.call-start = ((), (), s32[]{:S(2)}) async-start(), calls=%async_computation.11 | async-start | bytes 7864320 | tf_op jit(solution)/shard_map/all_gather | solution.py:96
  114.3 648.7 %reduce-scatter.6.cloned.1.call-start = ((), (), s32[]{:S(2)}) async-start(), calls=%async_computation.12 | async-start | bytes 2359296 | tf_op jit(solution)/shard_map/reduce_scatter | solution.py:230
  268.4 61.7 %copy-start.37 = (f32[1024]{0:T(1024)S(1)}, f32[1024]{0:T(1024)}, u32[]{:S(2)}) copy-start(f32[1024]{0:T(1024)} %param.29) | copy-start | bytes 12292
  671.8 6.5 copy-start.1
  678.3 7.5 copy-start.22
  678.3 7.5 copy-start.24
  680.5 6.3 copy-start.7
  723.6 84.5 %reduce-scatter.8.cloned.1.call-start = ((), (), s32[]{:S(2)}) async-start(), calls=%async_computation.13 | async-start | bytes 2359296 | tf_op jit(solution)/shard_map/reduce_scatter | solution.py:236
  728.1 623.5 %reduce-scatter.10.cloned.1.call-start = ((), (), s32[]{:S(2)}) async-start(), calls=%async_computation.15 | async-start | bytes 39321600
  740.2 24.0 %copy-start.14 = (f32[128,8,128]{0,2,1:T(8,128)S(1)}, f32[128,8,128]{0,2,1:T(8,128)}, u32[]{:S(2)}) copy-start(f32[128,8,128]{0,2,1:T(8,128)} %copy-done.13) | copy-start | bytes 1572868
  809.1 7.1 slice-start
  809.2 7.1 slice-start.1
  836.0 515.6 %copy-start.19 = (bf16[128,3072]{1,0:T(8,128)(2,1)S(1)}, bf16[128,3072]{1,0:T(8,128)(2,1)}, u32[]{:S(2)}) copy-start(bf16[128,3072]{1,0:T(8,128)(2,1)} %get-tuple-element.406) | copy-start | bytes 2359300
  836.0 643.1 %all-reduce.8.cloned.1.call-start = ((), (), s32[]{:S(2)}) async-start(), calls=%async_computation.14 | async-start | bytes 15728640 | tf_op jit(solution)/shard_map/psum | solution.py:274
  1351.6 5.9 copy-start.15
  1351.6 5.9 copy-start.34
  1351.6 6.7 copy-start.16
  1351.6 6.7 copy-start.26
  1358.4 46.4 %copy-start.41 = (f32[128]{0:T(128)S(1)}, f32[128]{0:T(128)}, u32[]{:S(2)}) copy-start(f32[128]{0:T(128)} %copy-done.40) | copy-start | bytes 1540
  (32 other events, 96.7 us)
Sparse Core Ops, SparseCore 0:
  9.6 48.3 all-gather.9
  59.5 44.4 all-gather.13
  105.6 79.5 all-gather.17
  187.5 26.2 all-gather.11
  216.1 27.7 all-gather.15
  245.4 80.7 all-gather.19
  327.7 113.8 all-gather.23
  443.1 113.5 all-gather.21
  558.2 113.5 all-gather.25
  723.7 39.2 reduce-scatter.5
  766.9 41.0 reduce-scatter.7
  836.1 515.4 reduce-scatter.9
  1354.9 124.0 all-reduce.7
where the time goes:
time: 1510 us; the launch traced here: 1500 us
  waiting for transfers between devices  1230 us (81%)
  matrix products  88.8 us (6%)
  local copies, waits for them, and re-layouts  76.9 us (5%)
  blocking collectives  43.2 us (3%)
  other arithmetic  39.3 us (3%)
  between operations  16.1 us (1%)
    unnamed x14, waiting for transfers between devices  520 us
    all_gather x1, waiting for transfers between devices, on_device(): lax.all_gather(up_proj, 'fsdp', axis=0, tiled=True)  111 us
    all_gather x1, waiting for transfers between devices, on_device(): lax.all_gather(down_proj, 'fsdp', axis=0, tiled=True)  110 us
    all_gather x1, waiting for transfers between devices, on_device(): lax.all_gather(gate_proj, 'fsdp', axis=0, tiled=True)  110 us
    psum x1, waiting for transfers between devices, on_device(): owned = lax.psum(owned_term, 'ctx').astype(jnp.float32)  73.3 us
    all_gather x1, waiting for transfers between devices, on_device(): lax.all_gather(query_proj, 'fsdp', axis=0, tiled=True)  61.8 us
    all_gather x1, waiting for transfers between devices, on_device(): lax.all_gather(output_proj, 'fsdp', axis=0, tiled=True)  55.6 us
    all_gather x1, waiting for transfers between devices, on_device(): lax.all_gather(value_proj, 'fsdp', axis=0, tiled=True)  47.4 us
  transfers between devices with their start and end apart: 13, of which 13 were waited for; matrix products, arithmetic and copies ran while one was open for 7% of the time, Pallas kernels for 0%

commit v1 on v0

--- a/solution.py
+++ b/solution.py
@@ -1,3 +1,4 @@
+import functools
 import math
 import jax
 import jax.numpy as jnp
@@ -7,6 +8,23 @@
 NORM_EPS = 1e-06
 ROPE_BASE = 1000000.0
 MASKED = -1e30
+
+
+def mark_plane_for(view, mesh_name):
+    t_next = lax.axis_size(mesh_name)
+    e_now = lax.axis_index(mesh_name)
+    near, far_arr = (t_next, e_now)
+    odd, before = (view, 1)
+    while before < near:
+        val2 = lax.ppermute(odd, mesh_name, [(h, h ^ before) for h in range(near)])
+        mid_arr = jnp.concatenate([odd, val2], axis=0)
+        fresh = jnp.concatenate([val2, odd], axis=0)
+        odd = jnp.where(far_arr & before == 0, mid_arr, fresh)
+        before = 2 * before
+    return odd
+
+
+bring_edge_over_axis = functools.partial(mark_plane_for, mesh_name="fsdp")
 
 
 def rms_norm(values, gain_vec):
@@ -92,7 +110,7 @@
     )
     gate_w, upper_w, down_w = (
         lax.all_gather(gate_proj, "fsdp", axis=0, tiled=True),
-        lax.all_gather(up_proj, "fsdp", axis=0, tiled=True),
+        bring_edge_over_axis(up_proj),
         lax.all_gather(down_proj, "fsdp", axis=0, tiled=True),
     )
     inputs = hidden_in[0]

time: 1510 us -> 1480 us (0.980)
  waiting for transfers between devices: 1230 us -> 1200 us
    all_gather x1 -> x0, waiting for transfers between devices: 111 us -> none  [on_device(): lax.all_gather(up_proj, 'fsdp', axis=0, tiled=True)]
    ppermute x0 -> x2, waiting for transfers between devices: none -> 93.5 us  [mark_plane_for(): val2 = lax.ppermute(odd, mesh_name, [(h, h ^ before) for h in range(near)])]
    all_gather x1, waiting for transfers between devices: 61.8 us -> 0.01 us  [on_device(): lax.all_gather(query_proj, 'fsdp', axis=0, tiled=True)]
    all_gather x1, waiting for transfers between devices: 55.6 us -> 89.7 us  [on_device(): lax.all_gather(output_proj, 'fsdp', axis=0, tiled=True)]
    all_gather x1, waiting for transfers between devices: 110 us -> 130 us  [on_device(): lax.all_gather(down_proj, 'fsdp', axis=0, tiled=True)]
    unnamed x14 -> x13, waiting for transfers between devices: 520 us -> 519 us
  transfers between devices with their start and end apart: 13 -> 14, of which waited for: 13 -> 12; matrix products, arithmetic and copies ran while one was open for 7% -> 8% of each run, Pallas kernels for 0% -> 0%
where the time goes in v1:
time: 1480 us; the launch traced here: 1470 us
  waiting for transfers between devices  1200 us (81%)
  matrix products  90.7 us (6%)
  local copies, waits for them, and re-layouts  77.1 us (5%)
  blocking collectives  43.2 us (3%)
  other arithmetic  41.8 us (3%)
  between operations  16.5 us (1%)
    unnamed x13, waiting for transfers between devices  519 us
    all_gather x1, waiting for transfers between devices, on_device(): lax.all_gather(down_proj, 'fsdp', axis=0, tiled=True)  130 us
    all_gather x1, waiting for transfers between devices, on_device(): lax.all_gather(gate_proj, 'fsdp', axis=0, tiled=True)  110 us
    ppermute x2, waiting for transfers between devices, mark_plane_for(): val2 = lax.ppermute(odd, mesh_name, [(h, h ^ before) for h in range(near)])  93.5 us
    all_gather x1, waiting for transfers between devices, on_device(): lax.all_gather(output_proj, 'fsdp', axis=0, tiled=True)  89.7 us
    psum x1, waiting for transfers between devices, on_device(): owned = lax.psum(owned_term, 'ctx').astype(jnp.float32)  73.2 us
    all_gather x1, waiting for transfers between devices, on_device(): lax.all_gather(value_proj, 'fsdp', axis=0, tiled=True)  47.4 us
    psum x1, blocking collectives, on_device(): lax.psum((attn_gain_grad, query_gain_grad, key_gain_grad, mlp_gain_grad),...  43.2 us
  transfers between devices with their start and end apart: 14, of which 12 were waited for; matrix products, arithmetic and copies ran while one was open for 8% of the time, Pallas kernels for 0%

profile of v1, /device:TPU:0, one launch (start us, length us, event | category | flops | bytes accessed | tf_op | source)
XLA Modules:
  0.0 1474.8 jit_solution(10687016288496532972)
XLA Ops:
  10.6 47.4 %all-gather.9.cloned.1.call-done = bf16[1024,1024]{1,0:T(8,128)(2,1)} async-done(((bf16[256,1024]{1,0:T(8,128)(2,1)}), bf16[1024,1024]{1,0:T(8,128)(2,1)}) %all-gather.9.cloned.1.call-update) | async-done | bytes 2097168 | tf_op jit(solution)/shard_map/all_gather | solution.py:108
  63.2 40.9 %all-gather.13.cloned.1.call-done = bf16[1024,1024]{1,0:T(8,128)(2,1)} async-done(((bf16[256,1024]{1,0:T(8,128)(2,1)}), bf16[1024,1024]{1,0:T(8,128)(2,1)}) %all-gather.13.cloned.1.call-update) | async-done | bytes 2097168 | tf_op jit(solution)/shard_map/all_gather | solution.py:107
  104.0 3.9 copy.60
  114.2 8.8 gather_fusion
  123.1 93.5 %collective-permute-done = bf16[256,3072]{1,0:T(8,128)(2,1)} collective-permute-done((bf16[256,3072]{1,0:T(8,128)(2,1)}, bf16[256,3072]{1,0:T(8,128)(2,1)}, u32[]{:S(2)}, u32[]{:S(2)}) %collective-permute-start) | collective-permute-done | bytes 1572896 | tf_op jit(solution)/shard_map/ppermute | solution.py:19
  220.2 6.4 copy.62
  232.5 13.6 all-gather.11.cloned.1.call-done
  249.6 26.6 %all-gather.15.cloned.1.call-done = bf16[1024,1024]{1,0:T(8,128)(2,1)} async-done(((bf16[128,1024]{1,0:T(8,128)(2,1)}), bf16[1024,1024]{1,0:T(8,128)(2,1)}) %all-gather.15.cloned.1.call-update) | async-done | bytes 2097168 | tf_op jit(solution)/shard_map/all_gather | solution.py:156
  278.8 4.0 while.39
  282.8 17.5 %while.40 = (s32[]{:T(128)}, f32[128,8,2,128]{0,3,2,1:T(8,128)}, bf16[2,512,8,128]{3,2,1,0:T(8,128)(2,1)}, s32[2,512]{1,0:T(2,128)S(1)}, s32[128]{0:T(128)S(1)},...) while((s32[]{:T(128)}, f32[128,8,2,128]{0,3,2,1:T(8,128)}, ...), condition=%wide.region_8.9_spmd.clone, body=%wide.region_7.8_spmd.clone.sunk | while | flops 541655040 | bytes 9058947 | solution.py:191
  302.4 89.7 %all-gather.19.cloned.1.call-done = bf16[1024,2048]{1,0:T(8,128)(2,1)} async-done(((bf16[256,2048]{1,0:T(8,128)(2,1)}), bf16[1024,2048]{1,0:T(8,128)(2,1)}) %all-gather.19.cloned.1.call-update) | async-done | bytes 4194320 | tf_op jit(solution)/shard_map/all_gather | solution.py:109
  392.2 3.9 multiply_reduce_fusion.8
  397.0 130.1 %all-gather.23.cloned.1.call-done = bf16[1024,3072]{1,0:T(8,128)(2,1)} async-done(((bf16[256,3072]{1,0:T(8,128)(2,1)}), bf16[1024,3072]{1,0:T(8,128)(2,1)}) %all-gather.23.cloned.1.call-update) | async-done | bytes 6291472 | tf_op jit(solution)/shard_map/all_gather | solution.py:114
  527.1 5.0 fusion.77
  532.2 110.1 %all-gather.21.cloned.1.call-done = bf16[1024,3072]{1,0:T(8,128)(2,1)} async-done(((bf16[256,3072]{1,0:T(8,128)(2,1)}), bf16[1024,3072]{1,0:T(8,128)(2,1)}) %all-gather.21.cloned.1.call-update) | async-done | bytes 6291472 | tf_op jit(solution)/shard_map/all_gather | solution.py:112
  642.2 4.0 fusion.107
  646.3 7.3 multiply_convert_fusion
  655.8 6.4 multiply_reduce_fusion.4
  675.6 19.8 %while.41 = (s32[]{:T(128)}, f32[128,8,2,128]{0,3,2,1:T(8,128)}, bf16[2,512,8,128]{3,1,2,0:T(8,128)(2,1)}, bf16[2,512,8,128]{3,1,2,0:T(8,128)(2,1)}, bf16[2,512,...) while((s32[]{:T(128)}, f32[128,8,2,128]{0,3,2,1:T(8,128)}, ...), condition=%wide.region_12.13_spmd.clone, body=%wide.region_11.12_spmd.clone.sunk | while | flops 1354301440 | bytes 76774256 | solution.py:242
  707.6 4.3 convolution_convert_fusion.2
  712.0 4.5 convert_bitcast_fusion
  716.5 6.7 convolution_convert_fusion
  723.2 16.5 %reduce-scatter.6.cloned.1.call-done = bf16[128,1024]{1,0:T(8,128)(2,1)} async-done(((bf16[1024,1024]{1,0:T(8,128)(2,1)}), bf16[128,1024]{1,0:T(8,128)(2,1)}) %reduce-scatter.6.cloned.1.call-update) | async-done | bytes 262160 | tf_op jit(solution)/shard_map/reduce_scatter | solution.py:248
  742.0 42.6 %reduce-scatter.8.cloned.1.call-done = bf16[128,1024]{1,0:T(8,128)(2,1)} async-done(((bf16[1024,1024]{1,0:T(8,128)(2,1)}), bf16[128,1024]{1,0:T(8,128)(2,1)}) %reduce-scatter.8.cloned.1.call-update) | async-done | bytes 262160 | tf_op jit(solution)/shard_map/reduce_scatter | solution.py:254
  785.8 7.1 convolution_convert_fusion.1
  792.9 19.7 %pad_maximum_fusion = bf16[1024,15360]{1,0:T(8,128)(2,1)} fusion(bf16[1024,3072]{1,0:T(8,128)(2,1)S(1)} %bitcast.288, bf16[1024,6144]{1,0:T(8,128)(2,1)} %convolution_convert_fusion, bf16[1024,2048]{1,0:T(8,128)(2,1)} %convolution_convert_fusion.2, bf16[1024,4096]{1,0:T(8,128)(2,1)} %convolution_convert_fusion.1), kind=kLoop, calls=%fused_computation.60 | loop fusion | flops 125829120 | bytes 62914560 | tf_op jit(solution)/shard_map/concatenate | solution.py:287
  812.6 515.5 %reduce-scatter.10.cloned.1.call-done = bf16[256,15360]{1,0:T(8,128)(2,1)} async-done(((bf16[1024,15360]{1,0:T(8,128)(2,1)}), bf16[256,15360]{1,0:T(8,128)(2,1)}) %reduce-scatter.10.cloned.1.call-update) | async-done | bytes 7864336
  1328.2 5.8 fusion.51
  1338.1 43.2 %all-reduce.5 = (f32[1024]{0:T(1024)}, f32[128]{0:T(128)}, f32[128]{0:T(128)}, f32[1024]{0:T(1024)}) all-reduce(f32[1024]{0:T(1024)S(1)} %get-tuple-element.333, f32[128]{0:T(128)S(1)} %get-tuple-element.327, f32[128]{0:T(128)S(1)} %get-tuple-element.331, ...), channel_id=1, replica_groups=mesh['fsdp'=4,'ctx'=8] {'fsdp','ctx'}, use_global_device_ids=true, to_apply=%region_19.20 | all-reduce | flops 2304 | bytes 18432 | tf_op jit(solution)/shard_map/psum | solution.py:293
  1382.3 73.2 %all-reduce.8.cloned.1.call-done = bf16[256,15360]{1,0:T(8,128)(2,1)} async-done(((bf16[256,15360]{1,0:T(8,128)(2,1)}), bf16[256,15360]{1,0:T(8,128)(2,1)}) %all-reduce.8.cloned.1.call-update) | async-done | bytes 7864336 | tf_op jit(solution)/shard_map/psum | solution.py:292
  1458.2 4.4 fusion.105
  1463.6 4.1 fusion.104
  (248 shorter events, 112.2 us)
Async XLA Ops:
  7.2 53.8 %copy-start = (s32[8,2]{0,1:T(2,128)S(1)}, s32[8,2]{0,1:T(2,128)}, u32[]{:S(2)}) copy-start(s32[8,2]{0,1:T(2,128)} %param.21) | copy-start | bytes 196
  7.2 50.8 %all-gather.9.cloned.1.call-start = ((), (), s32[]{:S(2)}) async-start(), calls=%async_computation.3 | async-start | bytes 2621440 | tf_op jit(solution)/shard_map/all_gather | solution.py:108
  7.9 96.1 %all-gather.13.cloned.1.call-start = ((), (), s32[]{:S(2)}) async-start(), calls=%async_computation.5 | async-start | bytes 2621440 | tf_op jit(solution)/shard_map/all_gather | solution.py:107
  8.7 99.3 %copy-start.5 = (bf16[1,128,1024]{2,1,0:T(8,128)(2,1)S(1)}, bf16[1,128,1024]{2,1,0:T(8,128)(2,1)}, u32[]{:S(2)}) copy-start(bf16[1,128,1024]{2,1,0:T(8,128)(2,1)} %param.20) | copy-start | bytes 786436
  8.7 99.3 %copy-start.38 = (f32[1024]{0:T(1024)S(1)}, f32[1024]{0:T(1024)}, u32[]{:S(2)}) copy-start(f32[1024]{0:T(1024)} %param.22) | copy-start | bytes 12292
  8.7 211.5 %all-gather.17.cloned.1.call-start = ((), (), s32[]{:S(2)}) async-start(), calls=%async_computation.7 | async-start | bytes 5242880 | tf_op jit(solution)/shard_map/all_gather | solution.py:106
  9.4 236.6 %all-gather.11.cloned.1.call-start = ((), (), s32[]{:S(2)}) async-start(), calls=%async_computation.4 | async-start | bytes 2359296 | tf_op jit(solution)/shard_map/all_gather | solution.py:157
  10.6 52.3 %copy-start.42 = (f32[128]{0:T(128)}, f32[128]{0:T(128)S(1)}, u32[]{:S(2)}) copy-start(f32[128]{0:T(128)S(1)} %fusion.67) | copy-start | bytes 1540
  60.9 49.5 %copy-start.40 = (f32[128]{0:T(128)S(1)}, f32[128]{0:T(128)}, u32[]{:S(2)}) copy-start(f32[128]{0:T(128)} %param.27) | copy-start | bytes 1540
  60.9 215.3 %all-gather.15.cloned.1.call-start = ((), (), s32[]{:S(2)}) async-start(), calls=%async_computation.6 | async-start | bytes 2359296 | tf_op jit(solution)/shard_map/all_gather | solution.py:156
  111.5 280.7 %all-gather.19.cloned.1.call-start = ((), (), s32[]{:S(2)}) async-start(), calls=%async_computation.8 | async-start | bytes 5242880 | tf_op jit(solution)/shard_map/all_gather | solution.py:109
  112.1 104.6 %copy-start.33 = (bf16[256,3072]{1,0:T(8,128)(2,1)S(1)}, bf16[256,3072]{1,0:T(8,128)(2,1)}, u32[]{:S(2)}) copy-start(bf16[256,3072]{1,0:T(8,128)(2,1)} %param.31) | copy-start | bytes 4718596
  112.1 415.0 %all-gather.23.cloned.1.call-start = ((), (), s32[]{:S(2)}) async-start(), calls=%async_computation.10 | async-start | bytes 7864320 | tf_op jit(solution)/shard_map/all_gather | solution.py:114
  112.8 529.4 %all-gather.21.cloned.1.call-start = ((), (), s32[]{:S(2)}) async-start(), calls=%async_computation.9 | async-start | bytes 7864320 | tf_op jit(solution)/shard_map/all_gather | solution.py:112
  112.9 103.7 %collective-permute-start = (bf16[256,3072]{1,0:T(8,128)(2,1)}, bf16[256,3072]{1,0:T(8,128)(2,1)}, u32[]{:S(2)}, u32[]{:S(2)}) collective-permute-start(bf16[256,3072]{1,0:T(8,128)(2,1)} %param.31), channel_id=1, source_target_pairs={{0,8},{8,0},{16,24},{24,16},{1,9},{9,1},{17,25},{25,17},{2,10},{10... | collective-permute-start | bytes 4718600 | tf_op jit(solution)/shard_map/ppermute | solution.py:19
  113.6 626.2 %reduce-scatter.6.cloned.1.call-start = ((), (), s32[]{:S(2)}) async-start(), calls=%async_computation.11 | async-start | bytes 2359296 | tf_op jit(solution)/shard_map/reduce_scatter | solution.py:248
  220.2 426.0 %collective-permute-start.1 = (bf16[512,3072]{1,0:T(8,128)(2,1)}, bf16[512,3072]{1,0:T(8,128)(2,1)}, u32[]{:S(2)}, u32[]{:S(2)}) collective-permute-start(bf16[512,3072]{1,0:T(8,128)(2,1)} %maximum_select_fusion.1), channel_id=1, source_target_pairs={{0,16},{8,24},{16,0},{24,8},{1,17},{9,25},{17,1},{25,9},{2,18},{10... | collective-permute-start | bytes 9437192 | tf_op jit(solution)/shard_map/ppermute | solution.py:19
  300.3 95.8 %copy-start.39 = (f32[1024]{0:T(1024)S(1)}, f32[1024]{0:T(1024)}, u32[]{:S(2)}) copy-start(f32[1024]{0:T(1024)} %param.29) | copy-start | bytes 12292
  396.1 259.7 %copy-start.14 = (f32[128,1024]{1,0:T(8,128)}, f32[128,1024]{1,0:T(8,128)S(1)}, u32[]{:S(2)}) copy-start(f32[128,1024]{1,0:T(8,128)S(1)} %get-tuple-element.424) | copy-start | bytes 1572868
  642.2 11.4 slice-start
  646.2 7.4 slice-start.1
  653.6 8.7 copy-start.24
  653.6 8.7 copy-start.35
  655.8 7.7 copy-start.6
  700.3 84.3 %reduce-scatter.8.cloned.1.call-start = ((), (), s32[]{:S(2)}) async-start(), calls=%async_computation.12 | async-start | bytes 2359296 | tf_op jit(solution)/shard_map/reduce_scatter | solution.py:254
  703.9 624.3 %reduce-scatter.10.cloned.1.call-start = ((), (), s32[]{:S(2)}) async-start(), calls=%async_computation.14 | async-start | bytes 39321600
  716.5 24.4 %copy-start.11 = (f32[128,8,128]{0,2,1:T(8,128)S(1)}, f32[128,8,128]{0,2,1:T(8,128)}, u32[]{:S(2)}) copy-start(f32[128,8,128]{0,2,1:T(8,128)} %copy-done.10) | copy-start | bytes 1572868
  785.8 7.1 slice-start.2
  785.8 7.1 slice-start.3
  812.6 515.6 %copy-start.15 = (f32[128,1024]{1,0:T(8,128)S(1)}, f32[128,1024]{1,0:T(8,128)}, u32[]{:S(2)}) copy-start(f32[128,1024]{1,0:T(8,128)} %copy-done.14) | copy-start | bytes 1572868
  812.6 642.9 %all-reduce.8.cloned.1.call-start = ((), (), s32[]{:S(2)}) async-start(), calls=%async_computation.13 | async-start | bytes 15728640 | tf_op jit(solution)/shard_map/psum | solution.py:292
  1335.0 46.3 %copy-start.43 = (f32[128]{0:T(128)S(1)}, f32[128]{0:T(128)}, u32[]{:S(2)}) copy-start(f32[128]{0:T(128)} %copy-done.42) | copy-start | bytes 1540
  (37 other events, 122.7 us)
Sparse Core Ops, SparseCore 0:
  9.6 48.3 all-gather.8
  59.5 44.4 all-gather.12
  105.6 110.8 all-gather.16
  218.9 27.1 all-gather.10
  248.4 27.7 all-gather.14
  277.6 114.5 all-gather.18
  393.7 133.3 all-gather.22
  528.7 113.4 all-gather.20
  700.4 39.3 reduce-scatter.5
  743.5 41.1 reduce-scatter.7
  812.7 515.4 reduce-scatter.9
  1331.3 124.0 all-reduce.7
